TPU v7x, 256 devices: a whole 4x4x8 slice. The times are simulated.
256 devices in a mesh: sta: 64 (over y, z, core), tpl: 4 (over x).
Axes of the slice: x: 4, y: 4, z: 8, core: 2. Of those that a mesh axis runs over, the one named last changes fastest.
Arguments:
- records: bfloat16 [2048, 3, 1024], P(('sta', 'tpl')), may hold values from -180 to 180
- waveforms: bfloat16 [384, 64, 3, 256], P('tpl', 'sta'), may hold values from -54 to 54
- station_ids: int32 [384, 64], P('tpl', 'sta'), may hold values from 0 to 2047, as said below
- lag_steps: int32 [384, 64, 3], P('tpl', 'sta'), may hold values from 0 to 255
Outputs:
- network_stack: float32 [384, 512], P('tpl', 'sta')
Inputs may be any that keep to these rules, and one draw needn't show every extreme that they name: `station_ids`: stations fall into aligned blocks of 32 (block = station // 32). Within each group of 96 consecutive templates, for every slot, at most 3 templates place that slot in the same block. Slot j of a template lies in block (b + j // 8) mod 64, where b is the block of its slot 0, so at most 24 templates of a group have some slot in one block, a number that some block reaches in every group. The stations of one template are distinct.
All inputs are finite; a program needn't handle non-finite values.
Results may differ from a plain program's by a relative error of at most 0.0003.
Values may be sent and summed in bfloat16 or wider, within the bound.
No kernel may reach another device: no remote copies, remote signals or barrier semaphores. Data moves between devices by JAX's collectives and lax.ppermute only.
A program may use at most 64 MiB of HBM per device.

v0:
```python
import math

import jax
import jax.numpy as jnp
from jax import lax
from jax.sharding import PartitionSpec as P

MAXLAG = 256
WINDOW = 512


epsilon = 1e-05


def window_scales(station_rows, length, positions):
    row_count = station_rows.shape[0]
    squares = station_rows.astype(jnp.float32)
    squares = (squares * squares).reshape(row_count, 3, -1, 128)
    block_sums = jnp.sum(squares, axis=-1)
    prefix = jnp.cumsum(squares, axis=-1) - squares
    span_blocks = length // 128
    blocks_out = positions // 128
    window = block_sums[:, :, 0:blocks_out]
    window = window + block_sums[:, :, 1 : 1 + blocks_out]
    energy = (
        window[..., None]
        - prefix[:, :, :blocks_out]
        + prefix[:, :, span_blocks : span_blocks + blocks_out]
    )
    return jnp.sqrt(energy.reshape(row_count, 3, positions) / length + epsilon)


def toeplitz(wave_part):
    row_count = wave_part.shape[0]
    kernel_width = wave_part.shape[-1] + 128
    padded = jnp.concatenate([wave_part, jnp.zeros((row_count, 3, 128), wave_part.dtype)], axis=-1)
    tiled_rows = jnp.tile(padded, (1, 1, 128))[..., : 128 * (kernel_width - 1)].reshape(
        row_count, 3, 128, kernel_width - 1
    )
    return jnp.concatenate(
        [tiled_rows, jnp.zeros((row_count, 3, 128, 1), wave_part.dtype)], axis=-1
    )


def cut_window(series, offset):
    return lax.dynamic_slice_in_dim(series, offset, WINDOW)


def on_device(records, waveforms, station_ids, lag_steps):
    owners = lax.axis_size("sta")
    groups = waveforms.shape[0]
    length = waveforms.shape[-1]
    block_stations = records.shape[0] * lax.axis_size("tpl")
    capacity = (groups + owners - 1) // owners + 1
    slots_all = owners * capacity
    positions = WINDOW + MAXLAG
    stations = station_ids[:, 0]
    owner_index = stations // block_stations
    member_marks = (owner_index[:, None] == jnp.arange(owners, dtype=jnp.int32)[None, :]).astype(
        jnp.int32
    )
    before = jnp.cumsum(member_marks, axis=0) - member_marks
    places = owner_index * capacity + jnp.sum(before * member_marks, axis=1)
    details = jnp.concatenate(
        [
            (stations - owner_index * block_stations)[:, None],
            jnp.arange(groups, dtype=jnp.int32)[:, None],
            lag_steps[:, 0, :],
        ],
        axis=1,
    )
    send_waves = jnp.zeros((slots_all, 3, length), waveforms.dtype).at[places].set(waveforms[:, 0])
    send_details = jnp.full((slots_all, 5), -1, jnp.int32).at[places].set(details)
    got_waves, got_details = (
        lax.all_to_all(
            send_waves.reshape(owners, capacity, 3, length),
            "sta",
            split_axis=0,
            concat_axis=0,
            tiled=True,
        ),
        lax.all_to_all(
            send_details.reshape(owners, capacity, 5),
            "sta",
            split_axis=0,
            concat_axis=0,
            tiled=True,
        ),
    )
    gathered = lax.all_gather(records, "tpl", axis=0, tiled=True)
    scales = window_scales(gathered, length, positions)
    blocks_all = gathered.shape[-1] // 128
    span_blocks = length // 128
    blocks_out = blocks_all - span_blocks
    framed = gathered.reshape(block_stations, 3, blocks_all, 128)
    stacked = jnp.concatenate(
        [framed[:, :, offset : offset + blocks_out] for offset in range(span_blocks + 1)], axis=-1
    )
    group_size = math.gcd(slots_all, 32)
    turn_count = slots_all // group_size
    got_waves = got_waves.reshape(turn_count, group_size, 3, length)
    got_details = got_details.reshape(turn_count, group_size, 5)
    template_ids = jnp.arange(groups, dtype=jnp.int32)

    def accumulate(running, block_items):
        wave_part, details_part = block_items
        local_rows = jnp.clip(details_part[:, 0], 0, block_stations - 1)
        frames = jnp.take(stacked, local_rows, axis=0)
        kernels = toeplitz(wave_part)
        raw_terms = jnp.einsum(
            "ectr,ecur->ectu", frames, kernels, preferred_element_type=jnp.float32
        ).reshape(group_size, 3, positions)
        wide_waves = wave_part.astype(jnp.float32)
        template_scale = jnp.sqrt(jnp.mean(wide_waves * wide_waves, axis=-1) + epsilon)
        normed = raw_terms / (
            length * jnp.take(scales, local_rows, axis=0) * template_scale[..., None]
        )
        shifted = jax.vmap(jax.vmap(cut_window))(normed, details_part[:, 2:5])
        summed = jnp.sum(shifted, axis=1)
        select = (template_ids[:, None] == details_part[None, :, 1]).astype(jnp.float32)
        return (
            running
            + jnp.dot(
                select, summed, precision=lax.Precision.HIGHEST, preferred_element_type=jnp.float32
            ),
            None,
        )

    network_stack, unused = lax.scan(
        accumulate, jnp.zeros((groups, WINDOW), jnp.float32), (got_waves, got_details)
    )
    piece_width = WINDOW // owners
    whole_sum = lax.psum(network_stack, "sta")
    return lax.dynamic_slice_in_dim(whole_sum, lax.axis_index("sta") * piece_width, piece_width, 1)


def solution(mesh):
    in_specs = (
        P(("sta", "tpl"), None, None),
        P("tpl", "sta", None, None),
        P("tpl", "sta"),
        P("tpl", "sta", None),
    )
    out_specs = P("tpl", "sta")
    return jax.shard_map(
        on_device, mesh=mesh, in_specs=in_specs, out_specs=out_specs, check_vma=False
    )
```

profile of v0, /device:TPU:1, one launch (start us, length us, event | category | flops | bytes accessed | tf_op | source)
XLA Modules:
  0.0 2165.4 jit_solution(6442156001963198578)
XLA Ops:
  10.0 13.2 all-to-all-start
  23.1 10.4 all_gather.3
  39.5 12.6 all-to-all-start.1
  52.4 27.0 %reduce_window_sum.23 = f32[32,3,8,128]{3,2,1,0:T(8,128)S(1)} reduce-window(f32[32,3,8,128]{3,2,1,0:T(8,128)S(1)} %copy.51, f32[]{:T(128)} %constant.74.clone.1), window={size=1x1x1x128 pad=0_0x0_0x0_0x127_0}, to_apply=%region_5.6 | reduce-window | flops 12484608 | bytes 786436 | tf_op jit(solution)/shard_map/jit(cumsum)/reduce_window_sum | solution.py:20
  80.5 1900.0 %while.18 = (s32[]{:T(128)}, f32[96,512]{1,0:T(8,128)S(1)}, s32[6,32,5]{1,2,0:T(8,128)S(1)}, bf16[32,3,6,384]{3,2,1,0:T(8,128)(2,1)S(1)}, bf16[6,32,3,256]{3,1,0...) while((s32[]{:T(128)}, f32[96,512]{1,0:T(8,128)S(1)}, ...), condition=%wide.region_9.10_spmd.clone.clone, body=%wide.region_6.9_spmd.clone.sunk.clone | while | flops 76150144 | bytes 80495904 | solution.py:129
  85.1 13.2 tile.16
  98.2 7.9 slice.117
  106.1 23.7 %reshape.141 = bf16[32,3,128,383]{3,2,0,1:T(8,128)(2,1)} reshape(bf16[32,3,49024]{2,0,1:T(8,128)(2,1)} %slice.117) | data formatting | bytes 18825216 | tf_op jit(solution)/shard_map/while/body/eval_jaxpr/reshape | solution.py:37
  130.6 5.9 fusion.34
  138.0 258.6 %while.17 = (s32[]{:T(128)}, f32[32,3,768]{2,1,0:T(4,128)S(1)}, s32[96,3]{0,1:T(4,128)S(1)}, f32[96,512]{1,0:T(8,128)S(1)}, s32[]{:T(128)}, /*index=5*/s32[]{:T(128)}) while((s32[]{:T(128)}, f32[32,3,768]{2,1,0:T(4,128)S(1)}, s32[96,3]{0,1:T(4,128)S(1)}, f32[96,512]{1,0:T(8,128)S(1)}, s32[]{:T(128)}, /*index=5*/s32[]{:T(128)}) %tuple.61), condition=%wide.while_cond, body=%wide.while_body.sunk | while | flops 2 | bytes 8337 | solution.py:46
  401.7 13.2 tile.16
  414.9 7.9 slice.117
  422.8 23.7 %reshape.141 = bf16[32,3,128,383]{3,2,0,1:T(8,128)(2,1)} reshape(bf16[32,3,49024]{2,0,1:T(8,128)(2,1)} %slice.117) | data formatting | bytes 18825216 | tf_op jit(solution)/shard_map/while/body/eval_jaxpr/reshape | solution.py:37
  454.7 258.6 %while.17 = (s32[]{:T(128)}, f32[32,3,768]{2,1,0:T(4,128)S(1)}, s32[96,3]{0,1:T(4,128)S(1)}, f32[96,512]{1,0:T(8,128)S(1)}, s32[]{:T(128)}, /*index=5*/s32[]{:T(128)}) while((s32[]{:T(128)}, f32[32,3,768]{2,1,0:T(4,128)S(1)}, s32[96,3]{0,1:T(4,128)S(1)}, f32[96,512]{1,0:T(8,128)S(1)}, s32[]{:T(128)}, /*index=5*/s32[]{:T(128)}) %tuple.61), condition=%wide.while_cond, body=%wide.while_body.sunk | while | flops 2 | bytes 8337 | solution.py:46
  718.4 13.2 tile.16
  731.5 7.9 slice.117
  739.5 23.7 %reshape.141 = bf16[32,3,128,383]{3,2,0,1:T(8,128)(2,1)} reshape(bf16[32,3,49024]{2,0,1:T(8,128)(2,1)} %slice.117) | data formatting | bytes 18825216 | tf_op jit(solution)/shard_map/while/body/eval_jaxpr/reshape | solution.py:37
  771.4 258.6 %while.17 = (s32[]{:T(128)}, f32[32,3,768]{2,1,0:T(4,128)S(1)}, s32[96,3]{0,1:T(4,128)S(1)}, f32[96,512]{1,0:T(8,128)S(1)}, s32[]{:T(128)}, /*index=5*/s32[]{:T(128)}) while((s32[]{:T(128)}, f32[32,3,768]{2,1,0:T(4,128)S(1)}, s32[96,3]{0,1:T(4,128)S(1)}, f32[96,512]{1,0:T(8,128)S(1)}, s32[]{:T(128)}, /*index=5*/s32[]{:T(128)}) %tuple.61), condition=%wide.while_cond, body=%wide.while_body.sunk | while | flops 2 | bytes 8337 | solution.py:46
  1035.1 13.2 tile.16
  1048.2 7.9 slice.117
  1056.1 23.7 %reshape.141 = bf16[32,3,128,383]{3,2,0,1:T(8,128)(2,1)} reshape(bf16[32,3,49024]{2,0,1:T(8,128)(2,1)} %slice.117) | data formatting | bytes 18825216 | tf_op jit(solution)/shard_map/while/body/eval_jaxpr/reshape | solution.py:37
  1080.6 5.9 fusion.34
  1088.0 258.6 %while.17 = (s32[]{:T(128)}, f32[32,3,768]{2,1,0:T(4,128)S(1)}, s32[96,3]{0,1:T(4,128)S(1)}, f32[96,512]{1,0:T(8,128)S(1)}, s32[]{:T(128)}, /*index=5*/s32[]{:T(128)}) while((s32[]{:T(128)}, f32[32,3,768]{2,1,0:T(4,128)S(1)}, s32[96,3]{0,1:T(4,128)S(1)}, f32[96,512]{1,0:T(8,128)S(1)}, s32[]{:T(128)}, /*index=5*/s32[]{:T(128)}) %tuple.61), condition=%wide.while_cond, body=%wide.while_body.sunk | while | flops 2 | bytes 8337 | solution.py:46
  1351.7 13.2 tile.16
  1364.9 7.9 slice.117
  1372.8 23.7 %reshape.141 = bf16[32,3,128,383]{3,2,0,1:T(8,128)(2,1)} reshape(bf16[32,3,49024]{2,0,1:T(8,128)(2,1)} %slice.117) | data formatting | bytes 18825216 | tf_op jit(solution)/shard_map/while/body/eval_jaxpr/reshape | solution.py:37
  1404.7 258.6 %while.17 = (s32[]{:T(128)}, f32[32,3,768]{2,1,0:T(4,128)S(1)}, s32[96,3]{0,1:T(4,128)S(1)}, f32[96,512]{1,0:T(8,128)S(1)}, s32[]{:T(128)}, /*index=5*/s32[]{:T(128)}) while((s32[]{:T(128)}, f32[32,3,768]{2,1,0:T(4,128)S(1)}, s32[96,3]{0,1:T(4,128)S(1)}, f32[96,512]{1,0:T(8,128)S(1)}, s32[]{:T(128)}, /*index=5*/s32[]{:T(128)}) %tuple.61), condition=%wide.while_cond, body=%wide.while_body.sunk | while | flops 2 | bytes 8337 | solution.py:46
  1668.4 13.2 tile.16
  1681.5 7.9 slice.117
  1689.4 23.7 %reshape.141 = bf16[32,3,128,383]{3,2,0,1:T(8,128)(2,1)} reshape(bf16[32,3,49024]{2,0,1:T(8,128)(2,1)} %slice.117) | data formatting | bytes 18825216 | tf_op jit(solution)/shard_map/while/body/eval_jaxpr/reshape | solution.py:37
  1721.3 258.6 %while.17 = (s32[]{:T(128)}, f32[32,3,768]{2,1,0:T(4,128)S(1)}, s32[96,3]{0,1:T(4,128)S(1)}, f32[96,512]{1,0:T(8,128)S(1)}, s32[]{:T(128)}, /*index=5*/s32[]{:T(128)}) while((s32[]{:T(128)}, f32[32,3,768]{2,1,0:T(4,128)S(1)}, s32[96,3]{0,1:T(4,128)S(1)}, f32[96,512]{1,0:T(8,128)S(1)}, s32[]{:T(128)}, /*index=5*/s32[]{:T(128)}) %tuple.61), condition=%wide.while_cond, body=%wide.while_body.sunk | while | flops 2 | bytes 8337 | solution.py:46
  1981.3 176.0 %all-reduce.4.cloned.1.call-done = f32[96,512]{0,1:T(8,128)} async-done(((f32[96,512]{0,1:T(8,128)}), f32[96,512]{0,1:T(8,128)}) %all-reduce.4.cloned.1.call-update) | async-done | bytes 196624 | tf_op jit(solution)/shard_map/psum | solution.py:133
  (2485 shorter events, 1617.3 us)
Async XLA Ops:
  10.0 29.6 %all-to-all-start = ((s32[64,3,5]{2,1,0:T(4,128)}), s32[64,3,5]{2,1,0:T(4,128)S(1)}, u32[]{:S(2)}, u32[]{:S(2)}) async-start(s32[64,3,5]{2,1,0:T(4,128)} %reshape.116), calls=%async_computation | async-start | bytes 262144 | tf_op jit(solution)/shard_map/all_to_all | solution.py:82
  39.5 40.5 %all-to-all-start.1 = ((bf16[64,3,3,256]{3,1,2,0:T(4,128)(2,1)}), bf16[64,3,3,256]{3,1,2,0:T(4,128)(2,1)S(1)}, u32[]{:S(2)}, u32[]{:S(2)}) async-start(bf16[64,3,3,256]{3,1,2,0:T(4,128)(2,1)} %copy.48), calls=%async_computation.1 | async-start | bytes 786432 | tf_op jit(solution)/shard_map/all_to_all | solution.py:75
  52.2 2105.1 %all-reduce.4.cloned.1.call-start = ((), (), s32[]{:S(2)}) async-start(), calls=%async_computation.2 | async-start | bytes 524288 | tf_op jit(solution)/shard_map/psum | solution.py:133
Sparse Core Ops, SparseCore 0:
  1981.4 175.8 all-reduce.3
where the time goes:
time: 2180 us; the launch traced here: 2170 us
  local copies, waits for them, and re-layouts  1860 us (85%)
  waiting for transfers between devices  176 us (8%)
  matrix products  36.7 us (2%)
  other arithmetic  32.4 us (1%)
  starting transfers between devices  25.8 us (1%)
    gather x2304, local copies, waits for them, and re-layouts  1540 us
    psum x1, waiting for transfers between devices, on_device(): whole_sum = lax.psum(network_stack, 'sta')  176 us
    reshape x6, local copies, waits for them, and re-layouts, toeplitz(): jnp.tile(padded, (1, 1, 128))[..., :128 * (kernel_width - 1)]  142 us
    another operation x12, local copies, waits for them, and re-layouts, toeplitz(): jnp.tile(padded, (1, 1, 128))[..., :128 * (kernel_width - 1)]  106 us
    slice x6, local copies, waits for them, and re-layouts, toeplitz(): jnp.tile(padded, (1, 1, 128))[..., :128 * (kernel_width - 1)]  47.5 us
  transfers between devices with their start and end apart: 3, of which 1 were waited for; matrix products, arithmetic and copies ran while one was open for 2% of the time, Pallas kernels for 0%

commit v1 on v0

v1 whole, which is shorter than its diff:
```python
import functools

import jax
import jax.numpy as jnp
from jax import lax
from jax.experimental import pallas as pl
from jax.experimental.pallas import tpu as pltpu
from jax.sharding import PartitionSpec as P

WINDOW = 512
EPSILON = 1e-05
BLOCKS = 64
STATIONS = 32
OWNERS = 4
PER_OWNER = STATIONS // OWNERS
GROUP = 96
CAP = 3
STEPS = 8
CHANNELS = 3
TLEN = 256
POSITIONS = 768
SAMPLES = 1024
ENTRIES = BLOCKS * CAP
ROWS = 32
PARTS = POSITIONS // 128
F32, BF16, I32 = jnp.float32, jnp.bfloat16, jnp.int32


def iota(shape, axis):
    return lax.broadcasted_iota(I32, shape, axis)


def ones_where(mask):
    return jnp.where(mask, 1.0, 0.0).astype(BF16)


def mm(left, right):
    return jnp.dot(left, right, preferred_element_type=F32)


def routing(block):
    hot = iota((BLOCKS, GROUP), 0) == block
    earlier = ones_where(iota((GROUP, GROUP), 0) < iota((GROUP, GROUP), 1))
    return hot, mm(ones_where(hot), earlier)


def pack_kernel(ids_ref, lag_ref, wave_ref, out_ref, rows_ref):
    me = lax.axis_index("tpl")
    ids = ids_ref[...]
    block = ids >> 5
    within = ids & (STATIONS - 1)
    label = ((me + OWNERS - (within >> 3)) & (OWNERS - 1)) * PER_OWNER + (within & (PER_OWNER - 1))
    hot, count = routing(block)
    kind = iota((128, GROUP), 0)
    details = jnp.where(kind == 0, label, 0)
    for channel in range(CHANNELS):
        details = jnp.where(kind == channel + 1, lag_ref[channel], details)
    details = details.astype(F32).astype(BF16)
    flip = ones_where(iota((TLEN, TLEN), 0) + iota((TLEN, TLEN), 1) == TLEN - 1)
    waves = [mm(wave_ref[channel], flip).astype(BF16) for channel in range(CHANNELS)]
    for c in range(CAP):
        pick = ones_where(hot & (count == float(c)))
        for channel in range(CHANNELS):
            part = mm(pick, waves[channel])
            for half in range(2):
                rows_ref[pl.ds(8 * c + 2 * channel + half, BLOCKS, stride=8 * CAP), :] = part[
                    :, 128 * half : 128 * half + 128
                ]
        rows_ref[pl.ds(8 * c + 6, BLOCKS, stride=8 * CAP), :] = lax.dot_general(
            pick, details, (((1,), (1,)), ((), ())), preferred_element_type=F32
        )
        rows_ref[pl.ds(8 * c + 7, BLOCKS, stride=8 * CAP), :] = jnp.zeros((BLOCKS, 128), F32)
    out_ref[...] = rows_ref[...].astype(BF16).reshape(BLOCKS, 8 * CAP, 128)


def correlate_kernel(
    got_ref,
    *refs,
):
    pieces = refs[:OWNERS]
    out_ref = refs[OWNERS]
    rows_ref, meta_ref, meta_smem, wave_ref, rec_ref, inv_ref, hankel_ref, raw_ref, scale_ref, acc_ref, sem = refs[OWNERS + 1 :]
    rows_ref[...] = got_ref[...].astype(F32).reshape(ENTRIES * 8, 128)

    details = rows_ref[pl.ds(6, ENTRIES, stride=8), :]
    details = jnp.concatenate([details, jnp.zeros((64, 128), F32)], axis=0).T
    meta_ref[...] = details[0:8].astype(I32)
    copy = pltpu.make_async_copy(meta_ref, meta_smem, sem)
    copy.start()

    entry = iota((1, ENTRIES), 1)
    source = entry // CAP
    key = details[0:1, :ENTRIES].astype(I32) * ROWS + (source >> 3) * 4 + (entry - source * CAP)
    select = ones_where(iota((STATIONS * ROWS, ENTRIES), 0) == key)
    for channel in range(CHANNELS):
        wave = jnp.concatenate(
            [rows_ref[pl.ds(2 * channel + half, ENTRIES, stride=8), :] for half in range(2)], axis=1
        )
        power = jnp.sum(wave * wave, axis=1, keepdims=True)
        scale = lax.rsqrt(power * (1.0 / TLEN) + EPSILON) * (1.0 / TLEN)
        scale_ref[channel] = jnp.broadcast_to(scale, (ENTRIES, 128))
        wave_ref[channel] = mm(select, wave.astype(BF16)).astype(BF16)

    delta = iota((2 * TLEN, TLEN), 0) - iota((2 * TLEN, TLEN), 1)
    band = ones_where((delta >= 0) & (delta < TLEN))
    for channel in range(CHANNELS):
        rec = jnp.concatenate([piece[channel].astype(F32) for piece in pieces], axis=0)
        rec_ref[channel * STATIONS : channel * STATIONS + STATIONS, :] = rec
        squares = rec * rec
        high = squares.astype(BF16)
        low = (squares - high.astype(F32)).astype(BF16)
        for part in range(POSITIONS // TLEN):
            lanes = slice(part * TLEN, part * TLEN + 2 * TLEN)
            energy = mm(high[:, lanes], band) + mm(low[:, lanes], band)
            inv_ref[channel * STATIONS : channel * STATIONS + STATIONS, part * TLEN : part * TLEN + TLEN] = lax.rsqrt(
                energy * (1.0 / TLEN) + EPSILON
            )

    def station_step(station, carry):
        for channel in range(CHANNELS):
            row = channel * STATIONS + station
            series = jnp.broadcast_to(rec_ref[pl.ds(row, 1), :], (16, SAMPLES))
            base = pltpu.roll(series, 1, 1, stride=1, stride_axis=0)
            for group in range(8):
                moved = (base if group == 0 else pltpu.roll(base, 16 * group, 1)).astype(BF16)
                hankel_ref[channel, 16 * group : 16 * group + 16, :] = moved[:, 256:]
                hankel_ref[channel, 128 + 16 * group : 128 + 16 * group + 16, :] = moved[:, 128:896]
            left = wave_ref[channel, pl.ds(pl.multiple_of(station * ROWS, ROWS), ROWS), :]
            raw = mm(left, hankel_ref[channel]) * inv_ref[pl.ds(row, 1), :]
            for part in range(PARTS):
                start = pl.multiple_of((row * PARTS + part) * ROWS, ROWS)
                raw_ref[pl.ds(start, ROWS), :] = raw[:, 128 * part : 128 * part + 128]
        return carry

    lax.fori_loop(0, STATIONS, station_step, 0)
    copy.wait()
    acc_ref[...] = jnp.zeros_like(acc_ref)
    lane = iota((4, 128), 1)

    def template_step(index, carry):
        step = index // CAP
        c = index - step * CAP
        place = step * 4 + c
        total = jnp.zeros((4, 128), F32)
        for slot in range(8):
            e = (step * 8 + slot) * CAP + c
            station = meta_smem[0, e]
            for channel in range(CHANNELS):
                lag = meta_smem[channel + 1, e]
                fine = lag & 127
                start = ((channel * STATIONS + station) * PARTS + (lag >> 7)) * ROWS + place
                here = raw_ref[pl.ds(start, 4, stride=ROWS), :]
                beyond = raw_ref[pl.ds(start + ROWS, 4, stride=ROWS), :]
                joined = jnp.where(lane >= fine, here, beyond) * scale_ref[channel, pl.ds(e, 1), :]
                total = total + pltpu.roll(joined, (128 - fine) & 127, 1)
        acc_ref[pl.ds(place, 4, stride=ROWS), :] = total
        return carry

    lax.fori_loop(0, STEPS * CAP, template_step, 0)
    acc_ref[...] = acc_ref[...].T
    quarter = iota((16, 128), 1) >> 5
    for half in range(2):
        columns = [acc_ref[pl.ds(4 * half + low, 16, stride=8), :] for low in range(4)]
        for part in range(4):
            joined = None
            for low in range(4):
                shift = (32 * (low - part)) % 128
                moved = columns[low] if shift == 0 else pltpu.roll(columns[low], shift, 1)
                joined = moved if joined is None else jnp.where(quarter == low, moved, joined)
            out_ref[16 * part : 16 * part + 16, half, :] = joined


def unpack_kernel(ids_ref, got_ref, out_ref, twice_ref):
    shift = lax.axis_index("sta") >> 3
    block = ((ids_ref[...] >> 5) + BLOCKS - shift) & (BLOCKS - 1)
    hot, count = routing(block)
    hot = jnp.where(hot, 1.0, 0.0)
    rank = jnp.sum(hot * count, axis=0, keepdims=True)
    step = (iota((BLOCKS, 128), 1) >> 2) & 7
    keep = (iota((128, GROUP), 0) & 3).astype(F32) == rank
    for half in range(2):
        twice_ref[0:BLOCKS, :] = got_ref[:, half, :]
        twice_ref[BLOCKS : 2 * BLOCKS, :] = got_ref[:, half, :]
        aligned = twice_ref[0:BLOCKS, :]
        for d in range(1, STEPS):
            aligned = jnp.where(step == d, twice_ref[d : d + BLOCKS, :], aligned)
        picked = jnp.dot(aligned.T, hot, precision=lax.Precision.HIGHEST, preferred_element_type=F32)
        picked = jnp.where(keep, picked, 0.0)
        for low in range(4):
            out_ref[4 * half + low : 4 * half + low + 1, :] = jnp.sum(
                picked[32 * low : 32 * low + 32], axis=0, keepdims=True
            )


VMEM = pl.BlockSpec(memory_space=pltpu.VMEM)


def on_device(records, waveforms, station_ids, lag_steps):
    ids = station_ids.T
    own = records.transpose(1, 0, 2)
    pieces = [own] + [
        lax.ppermute(own, "tpl", [(i, (i + hop) % OWNERS) for i in range(OWNERS)])
        for hop in range(1, OWNERS)
    ]
    send = pl.pallas_call(
        pack_kernel,
        out_shape=jax.ShapeDtypeStruct((BLOCKS, 8 * CAP, 128), BF16),
        in_specs=[VMEM] * 3,
        out_specs=VMEM,
        scratch_shapes=[pltpu.VMEM((BLOCKS * 8 * CAP, 128), F32)],
        name="pack",
    )(ids, lag_steps.transpose(2, 1, 0), waveforms[:, 0].transpose(1, 0, 2))
    got = lax.all_to_all(send, "sta", split_axis=0, concat_axis=0, tiled=True)
    stacks = pl.pallas_call(
        correlate_kernel,
        out_shape=jax.ShapeDtypeStruct((BLOCKS, 2, 128), F32),
        in_specs=[VMEM] * (1 + OWNERS),
        out_specs=VMEM,
        scratch_shapes=[
            pltpu.VMEM((ENTRIES * 8, 128), F32),
            pltpu.VMEM((8, 256), I32),
            pltpu.SMEM((8, 256), I32),
            pltpu.VMEM((CHANNELS, STATIONS * ROWS, TLEN), BF16),
            pltpu.VMEM((CHANNELS * STATIONS, SAMPLES), F32),
            pltpu.VMEM((CHANNELS * STATIONS, POSITIONS), F32),
            pltpu.VMEM((CHANNELS, TLEN, POSITIONS), BF16),
            pltpu.VMEM((CHANNELS * STATIONS * PARTS * ROWS, 128), F32),
            pltpu.VMEM((CHANNELS, ENTRIES, 128), F32),
            pltpu.VMEM((128, 128), F32),
            pltpu.SemaphoreType.DMA,
        ],
        compiler_params=pltpu.CompilerParams(vmem_limit_bytes=40 << 20),
        name="correlate",
    )(got, *pieces)
    shared = lax.all_to_all(stacks, "sta", split_axis=0, concat_axis=0, tiled=True)
    out = pl.pallas_call(
        unpack_kernel,
        out_shape=jax.ShapeDtypeStruct((8, GROUP), F32),
        in_specs=[VMEM] * 2,
        out_specs=VMEM,
        scratch_shapes=[pltpu.VMEM((2 * BLOCKS, 128), F32)],
        name="unpack",
    )(ids, shared)
    return out.T


def solution(mesh):
    in_specs = (
        P(("sta", "tpl"), None, None),
        P("tpl", "sta", None, None),
        P("tpl", "sta"),
        P("tpl", "sta", None),
    )
    return jax.shard_map(
        on_device, mesh=mesh, in_specs=in_specs, out_specs=P("tpl", "sta"), check_vma=False
    )
```

time: 2180 us -> 71.7 us (0.03)
  local copies, waits for them, and re-layouts: 1860 us -> 0.01 us
  waiting for transfers between devices: 176 us -> 9.7 us
  matrix products: 36.7 us -> 0 us
  other arithmetic: 32.4 us -> 0 us
  Pallas kernels: 0 us -> 27.6 us
    gather x2334 -> x0, local copies, waits for them, and re-layouts: 1550 us -> none
    psum x1 -> x0, waiting for transfers between devices: 176 us -> none  [on_device(): whole_sum = lax.psum(network_stack, 'sta')]
    reshape x17 -> x0, local copies, waits for them, and re-layouts: 145 us -> none  [the longest x6 142 us: toeplitz(): jnp.tile(padded, (1, 1, 128))[..., :128 * (kernel_width - 1)]]
    another operation x12 -> x0, local copies, waits for them, and re-layouts: 106 us -> none  [toeplitz(): jnp.tile(padded, (1, 1, 128))[..., :128 * (kernel_width - 1)]]
    slice x7 -> x0, local copies, waits for them, and re-layouts: 47.6 us -> none  [the longest x6 47.5 us: toeplitz(): jnp.tile(padded, (1, 1, 128))[..., :128 * (kernel_width - 1)]]
    dot_general x12 -> x0, matrix products: 36.7 us -> none  [the longest x6 35.4 us: accumulate(): jnp.einsum('ectr,ecur->ectu', frames, kernels, preferred_element_type=jnp...]
    pallas_call x0 -> x3, Pallas kernels: none -> 27.6 us  [the longest x1 23.6 us: on_device(): pl.pallas_call(correlate_kernel, out_shape=jax.ShapeDtypeStruct((BLOCKS,...]
    another operation x2 -> x0, other arithmetic: 27.1 us -> none  [the longest x1 27 us: window_scales(): prefix = jnp.cumsum(squares, axis=-1) - squares]
  transfers between devices with their start and end apart: 3 -> 4, of which waited for: 1 -> 3; matrix products, arithmetic and copies ran while one was open for 2% -> 0% of each run, Pallas kernels for 0% -> 0%
where the time goes in v1:
time: 71.7 us; the launch traced here: 71.4 us
  Pallas kernels  27.6 us (38%)
  starting transfers between devices  18.2 us (25%)
  blocking collectives  15.9 us (22%)
  waiting for transfers between devices  9.7 us (14%)
    pallas_call x1, Pallas kernels, on_device(): pl.pallas_call(correlate_kernel, out_shape=jax.ShapeDtypeStruct((BLOCKS,...  23.6 us
    all_to_all x1, blocking collectives, on_device(): lax.all_to_all(stacks, 'sta', split_axis=0, concat_axis=0, tiled=True)  15.9 us
    all_to_all x1, starting transfers between devices, on_device(): got = lax.all_to_all(send, 'sta', split_axis=0, concat_axis=0, tiled=True)  13.3 us
    all_to_all x1, waiting for transfers between devices, on_device(): got = lax.all_to_all(send, 'sta', split_axis=0, concat_axis=0, tiled=True)  7.62 us
    ppermute x3, starting transfers between devices, on_device(): lax.ppermute(own, 'tpl', [(i, (i + hop) % OWNERS) for i in range(OWNERS)])  4.89 us
    pallas_call x1, Pallas kernels, on_device(): pl.pallas_call(pack_kernel, out_shape=jax.ShapeDtypeStruct((BLOCKS, 8 * C...  2.17 us
    ppermute x3, waiting for transfers between devices, on_device(): lax.ppermute(own, 'tpl', [(i, (i + hop) % OWNERS) for i in range(OWNERS)])  2.08 us
    pallas_call x1, Pallas kernels, on_device(): pl.pallas_call(unpack_kernel, out_shape=jax.ShapeDtypeStruct((8, GROUP),...  1.83 us
  transfers between devices with their start and end apart: 4, of which 3 were waited for; matrix products, arithmetic and copies ran while one was open for 0% of the time, Pallas kernels for 0%

profile of v1, /device:TPU:1, one launch (start us, length us, event | category | flops | bytes accessed | tf_op | source)
XLA Modules:
  0.0 71.4 jit_solution(10387971772919494834)
XLA Ops:
  0.0 2.2 %pack.1 = bf16[64,24,128]{2,1,0:T(8,128)(2,1)} custom-call(s32[1,96]{1,0:T(1,128)} %bitcast.12, s32[3,1,96]{2,1,0:T(1,128)} %bitcast.14, bf16[3,96,256]{2,1,0:T(8,128)(2,1)} %bitcast.11), custom_call_target="tpu_custom_call" | custom-call | tf_op jit(solution)/shard_map/pack/pallas_call | solution.py:205
  2.2 0.0 copy-start
  2.2 13.3 %all-to-all-start = ((bf16[64,24,128]{2,1,0:T(8,128)(2,1)}), bf16[64,24,128]{2,1,0:T(8,128)(2,1)S(1)}, u32[]{:S(2)}, u32[]{:S(2)}) async-start(bf16[64,24,128]{2,1,0:T(8,128)(2,1)} %pack.1), calls=%async_computation | async-start | bytes 786432 | tf_op jit(solution)/shard_map/all_to_all | solution.py:213
  15.5 0.0 copy-done
  15.5 1.3 %collective-permute-start = (bf16[3,8,1024]{2,1,0:T(8,128)(2,1)S(1)}, bf16[3,8,1024]{2,1,0:T(8,128)(2,1)S(1)}, u32[]{:S(2)}, u32[]{:S(2)}) collective-permute-start(bf16[3,8,1024]{2,1,0:T(8,128)(2,1)S(1)} %bitcast.7), channel_id=1, source_target_pairs={{0,1},{1,2},{2,3},{3,0},{4,5},{5,6},{6,7},{7,4},{8,9},{9,10},{10,1... | collective-permute-start | bytes 147464 | tf_op jit(solution)/shard_map/ppermute | solution.py:202
  16.8 2.5 %collective-permute-start.1 = (bf16[3,8,1024]{2,1,0:T(8,128)(2,1)S(1)}, bf16[3,8,1024]{2,1,0:T(8,128)(2,1)S(1)}, u32[]{:S(2)}, u32[]{:S(2)}) collective-permute-start(bf16[3,8,1024]{2,1,0:T(8,128)(2,1)S(1)} %bitcast.8), channel_id=1, source_target_pairs={{0,2},{1,3},{2,0},{3,1},{4,6},{5,7},{6,4},{7,5},{8,10},{9,11},{10,... | collective-permute-start | bytes 147464 | tf_op jit(solution)/shard_map/ppermute | solution.py:202
  19.2 1.2 %collective-permute-start.2 = (bf16[3,8,1024]{2,1,0:T(8,128)(2,1)S(1)}, bf16[3,8,1024]{2,1,0:T(8,128)(2,1)S(1)}, u32[]{:S(2)}, u32[]{:S(2)}) collective-permute-start(bf16[3,8,1024]{2,1,0:T(8,128)(2,1)S(1)} %bitcast.9), channel_id=1, source_target_pairs={{0,3},{1,0},{2,1},{3,2},{4,7},{5,4},{6,5},{7,6},{8,11},{9,8},{10,9... | collective-permute-start | bytes 147464 | tf_op jit(solution)/shard_map/ppermute | solution.py:202
  20.4 0.0 collective-permute-done.refs_1_
  20.4 1.3 %collective-permute-done.1.refs_2_ = bf16[3,8,1024]{2,1,0:T(8,128)(2,1)S(1)} collective-permute-done((bf16[3,8,1024]{2,1,0:T(8,128)(2,1)S(1)}, bf16[3,8,1024]{2,1,0:T(8,128)(2,1)S(1)}, u32[]{:S(2)}, u32[]{:S(2)}) %collective-permute-start.1) | collective-permute-done | bytes 49184 | tf_op jit(solution)/shard_map/ppermute | solution.py:202
  21.7 0.8 %collective-permute-done.2.refs_3_ = bf16[3,8,1024]{2,1,0:T(8,128)(2,1)S(1)} collective-permute-done((bf16[3,8,1024]{2,1,0:T(8,128)(2,1)S(1)}, bf16[3,8,1024]{2,1,0:T(8,128)(2,1)S(1)}, u32[]{:S(2)}, u32[]{:S(2)}) %collective-permute-start.2) | collective-permute-done | bytes 49184 | tf_op jit(solution)/shard_map/ppermute | solution.py:202
  22.5 7.6 %all-to-all-done.got_ref = bf16[64,24,128]{2,1,0:T(8,128)(2,1)S(1)} async-done(((bf16[64,24,128]{2,1,0:T(8,128)(2,1)}), bf16[64,24,128]{2,1,0:T(8,128)(2,1)S(1)}, u32[]{:S(2)}, u32[]{:S(2)}) %all-to-all-start) | async-done | bytes 393248 | tf_op jit(solution)/shard_map/all_to_all | solution.py:213
  30.1 23.6 %correlate.1 = f32[64,2,128]{2,1,0:T(2,128)S(1)} custom-call(bf16[64,24,128]{2,1,0:T(8,128)(2,1)S(1)} %all-to-all-done.got_ref, bf16[3,8,1024]{2,1,0:T(8,128)(2,1)S(1)} %bitcast.10, bf16[3,8,1024]{2,1,0:T(8,128)(2,1)S(1)} %collective-permute-done.refs_1_, bf16[3,8,1024]{2,1,0:T(8,128)(2,1)S(1)} %collective-permute-done.1.refs_2_, ...), custom_call_target="tpu_custom_call" | custom-call | tf_op jit(solution)/shard_map/correlate/pallas_call | solution.py:214
  53.7 15.9 %all_to_all.10.got_ref = f32[64,2,128]{2,1,0:T(2,128)} all-to-all(f32[64,2,128]{2,1,0:T(2,128)S(1)} %correlate.1), channel_id=1, replica_groups=mesh['sta'=64,'tpl'=4] {'sta'}, dimensions={0} | all-to-all | bytes 131072 | tf_op jit(solution)/shard_map/all_to_all | solution.py:235
  69.6 1.8 %unpack.1 = f32[8,96]{1,0:T(8,128)} custom-call(s32[1,96]{1,0:T(1,128)} %bitcast.13, f32[64,2,128]{2,1,0:T(2,128)} %all_to_all.10.got_ref), custom_call_target="tpu_custom_call" | custom-call | tf_op jit(solution)/shard_map/unpack/pallas_call | solution.py:236
Async XLA Ops:
  2.2 13.3 %copy-start = (bf16[8,3,1024]{2,0,1:T(8,128)(2,1)S(1)}, bf16[8,3,1024]{2,0,1:T(8,128)(2,1)}, u32[]{:S(2)}) copy-start(bf16[8,3,1024]{2,0,1:T(8,128)(2,1)} %param.4) | copy-start | bytes 147460
  2.2 27.9 %all-to-all-start = ((bf16[64,24,128]{2,1,0:T(8,128)(2,1)}), bf16[64,24,128]{2,1,0:T(8,128)(2,1)S(1)}, u32[]{:S(2)}, u32[]{:S(2)}) async-start(bf16[64,24,128]{2,1,0:T(8,128)(2,1)} %pack.1), calls=%async_computation | async-start | bytes 786432 | tf_op jit(solution)/shard_map/all_to_all | solution.py:213
  15.5 4.9 %collective-permute-start = (bf16[3,8,1024]{2,1,0:T(8,128)(2,1)S(1)}, bf16[3,8,1024]{2,1,0:T(8,128)(2,1)S(1)}, u32[]{:S(2)}, u32[]{:S(2)}) collective-permute-start(bf16[3,8,1024]{2,1,0:T(8,128)(2,1)S(1)} %bitcast.7), channel_id=1, source_target_pairs={{0,1},{1,2},{2,3},{3,0},{4,5},{5,6},{6,7},{7,4},{8,9},{9,10},{10,1... | collective-permute-start | bytes 147464 | tf_op jit(solution)/shard_map/ppermute | solution.py:202
  16.8 4.9 %collective-permute-start.1 = (bf16[3,8,1024]{2,1,0:T(8,128)(2,1)S(1)}, bf16[3,8,1024]{2,1,0:T(8,128)(2,1)S(1)}, u32[]{:S(2)}, u32[]{:S(2)}) collective-permute-start(bf16[3,8,1024]{2,1,0:T(8,128)(2,1)S(1)} %bitcast.8), channel_id=1, source_target_pairs={{0,2},{1,3},{2,0},{3,1},{4,6},{5,7},{6,4},{7,5},{8,10},{9,11},{10,... | collective-permute-start | bytes 147464 | tf_op jit(solution)/shard_map/ppermute | solution.py:202
  19.2 3.2 %collective-permute-start.2 = (bf16[3,8,1024]{2,1,0:T(8,128)(2,1)S(1)}, bf16[3,8,1024]{2,1,0:T(8,128)(2,1)S(1)}, u32[]{:S(2)}, u32[]{:S(2)}) collective-permute-start(bf16[3,8,1024]{2,1,0:T(8,128)(2,1)S(1)} %bitcast.9), channel_id=1, source_target_pairs={{0,3},{1,0},{2,1},{3,2},{4,7},{5,4},{6,5},{7,6},{8,11},{9,8},{10,9... | collective-permute-start | bytes 147464 | tf_op jit(solution)/shard_map/ppermute | solution.py:202
